TPU v7x, 1024 devices: a whole 4x4x32 slice. The times are simulated.
1024 devices in a mesh: ctx: 8 (over y, core), tp: 16 (over x, z_hi), section: 8 (over z_lo).
Axes of the slice: x: 4, y: 4, z: 32 (z_hi: 4, z_lo: 8; z = z_hi * 8 + z_lo), core: 2. Of those that a mesh axis runs over, the one named last changes fastest.
Arguments:
- queries: bfloat16 [2, 8192, 8192], P(None, ('ctx', 'section'), 'tp'), may hold values from -15 to 15
- self_kv: bfloat16 [2, 8192, 2048], P(None, ('ctx', 'section')), may hold values from -6 to 6
- image_kv: bfloat16 [1024, 2048], P(('ctx', 'tp', 'section')), may hold values from -6 to 6
- cross_gate: float32 [64], P('tp'), may hold values from 0.3 to 2
- lengths: int32 [2], replicated, may hold values from 2048 to 8192, as said below
Outputs:
- attended: bfloat16 [2, 8192, 8192], P(None, ('ctx', 'section'), 'tp')
Inputs may be any that keep to these rules, and one draw needn't show every extreme that they name: `lengths`: one of the two sequences uses all 8192 positions, the other fewer.
All inputs are finite; a program needn't handle non-finite values.
Results may differ from a plain program's by a relative error of at most 0.004.
Values may be sent and summed in bfloat16 or wider, within the bound.
A program may use at most 128 MiB of HBM per device.

v0:
```python
import math

import jax
import jax.numpy as jnp
from jax import lax
from jax.sharding import PartitionSpec as P

HQ = 64
KVH = 8
HEAD_SIZE = 128


neg_large = -1e30


def fold_block(carry_state, query_grid, key_matrix, value_matrix, allowed, score_form, value_form):
    row_best, row_total, weighted = carry_state
    logit_scores = jnp.einsum(
        score_form, query_grid, key_matrix, preferred_element_type=jnp.float32
    ) * (1.0 / math.sqrt(HEAD_SIZE))
    masked = jnp.where(allowed, logit_scores, neg_large)
    new_best = jnp.maximum(row_best, jnp.max(masked, axis=-1))
    weights = jnp.where(allowed, jnp.exp(masked - new_best[..., None]), 0.0)
    shrink = jnp.exp(row_best - new_best)
    row_total = row_total * shrink + jnp.sum(weights, axis=-1)
    weighted = weighted * shrink[..., None] + jnp.einsum(
        value_form, weights.astype(jnp.bfloat16), value_matrix, preferred_element_type=jnp.float32
    )
    return (new_best, row_total, weighted)


def finish(carry_state):
    return jnp.transpose(carry_state[2] / carry_state[1][..., None], (0, 3, 1, 2, 4))


def per_device(queries, self_kv, image_kv, cross_gate, lengths):
    tp_count = lax.axis_size("tp")
    heads_local = HQ // tp_count
    kv_local = max(1, KVH // tp_count)
    replicas = max(1, tp_count // KVH)
    heads_per_kv = heads_local // kv_local
    seq_rows = queries.shape[1]
    kv_cols = kv_local * 2 * HEAD_SIZE
    tp_rank = lax.axis_index("tp")
    own_pairs = lax.dynamic_slice_in_dim(self_kv, tp_rank // replicas * kv_cols, kv_cols, 2)
    query_grid = queries.reshape(2, seq_rows, kv_local, heads_per_kv, HEAD_SIZE)
    block_rank = lax.axis_index(("ctx", "section"))
    query_pos = block_rank * seq_rows + jnp.arange(seq_rows, dtype=jnp.int32)
    last_needed = jnp.minimum(block_rank * seq_rows + seq_rows - 1, jnp.max(lengths) - 1)
    start_state = (
        jnp.full((2, kv_local, heads_per_kv, seq_rows), neg_large, jnp.float32),
        jnp.zeros((2, kv_local, heads_per_kv, seq_rows), jnp.float32),
        jnp.zeros((2, kv_local, heads_per_kv, seq_rows, HEAD_SIZE), jnp.float32),
    )
    carry_state = start_state
    kv_piece = lax.all_gather(own_pairs, ("ctx", "section"), axis=1, tiled=True)
    row_count = kv_piece.shape[1]
    block_rows = math.gcd(row_count, 512)
    blocks = jnp.moveaxis(
        kv_piece.reshape(2, row_count // block_rows, block_rows, kv_local, 2, HEAD_SIZE), 1, 0
    )

    def self_one_block(inner_state, scan_item):
        block_number, block_pairs = scan_item
        block_first = block_number * block_rows
        key_pos = block_first + jnp.arange(block_rows, dtype=jnp.int32)
        allowed = (key_pos[None, None, :] <= query_pos[None, :, None]) & (
            key_pos[None, None, :] < lengths[:, None, None]
        )

        def compute_block(state_in):
            return fold_block(
                state_in,
                query_grid,
                block_pairs[:, :, :, 0],
                block_pairs[:, :, :, 1],
                allowed[:, None, None],
                "bsgrd,bpgd->bgrsp",
                "bgrsp,bpgd->bgrsd",
            )

        def keep_state(state_in):
            return state_in

        return (lax.cond(block_first > last_needed, keep_state, compute_block, inner_state), None)

    carry_state, _ = lax.scan(
        self_one_block, carry_state, (jnp.arange(row_count // block_rows, dtype=jnp.int32), blocks)
    )
    image_rows = image_kv.shape[0]
    copies = jnp.repeat(image_kv.reshape(image_rows, KVH // kv_local, kv_cols), replicas, axis=1)
    image_own = lax.all_to_all(
        copies.reshape(image_rows, tp_count * kv_cols),
        "tp",
        split_axis=1,
        concat_axis=0,
        tiled=True,
    )
    image_carry_state = start_state
    kv_piece = lax.all_gather(image_own, ("ctx", "section"), axis=0, tiled=True)
    row_count = kv_piece.shape[0]
    image_block_rows = math.gcd(row_count, 512)
    blocks = kv_piece.reshape(
        row_count // image_block_rows, image_block_rows, kv_local, 2, HEAD_SIZE
    )
    everywhere = jnp.ones((), jnp.bool_)

    def image_one_block(inner_state, block_pairs):
        return (
            fold_block(
                inner_state,
                query_grid,
                block_pairs[:, :, 0],
                block_pairs[:, :, 1],
                everywhere,
                "bsgrd,pgd->bgrsp",
                "bgrsp,pgd->bgrsd",
            ),
            None,
        )

    image_carry_state, _ = lax.scan(image_one_block, image_carry_state, blocks)
    gate_factor = jnp.tanh(cross_gate).reshape(1, 1, kv_local, heads_per_kv, 1)
    attended = finish(carry_state) + gate_factor * finish(image_carry_state)
    return attended.reshape(2, seq_rows, heads_local * HEAD_SIZE).astype(jnp.bfloat16)


def solution(mesh):
    placed = (
        P(None, ("ctx", "section"), "tp"),
        P(None, ("ctx", "section"), None),
        P(("ctx", "tp", "section"), None),
        P("tp"),
        P(),
    )
    return jax.shard_map(
        per_device,
        mesh=mesh,
        in_specs=placed,
        out_specs=P(None, ("ctx", "section"), "tp"),
        check_vma=False,
    )
```

profile of v0, /device:TPU:249, one launch (start us, length us, event | category | flops | bytes accessed | tf_op | source)
XLA Modules:
  0.0 409.6 jit_solution(15210069226128486884)
XLA Ops:
  11.1 23.1 %all-to-all-start = ((bf16[16,2,128]{2,1,0:T(2,128)(2,1)}), bf16[16,2,128]{2,1,0:T(2,128)(2,1)S(1)}, u32[]{:S(2)}, u32[]{:S(2)}) async-start(bf16[16,2,128]{2,1,0:T(2,128)(2,1)} %reshape.182), calls=%async_computation | async-start | bytes 16384 | tf_op jit(solution)/shard_map/all_to_all | solution.py:92
  38.2 19.2 %all-to-all-done = bf16[16,2,128]{2,1,0:T(2,128)(2,1)S(1)} async-done(((bf16[16,2,128]{2,1,0:T(2,128)(2,1)}), bf16[16,2,128]{2,1,0:T(2,128)(2,1)S(1)}, u32[]{:S(2)}, u32[]{:S(2)}) %all-to-all-start) | async-done | bytes 8224 | tf_op jit(solution)/shard_map/all_to_all | solution.py:92
  57.4 213.7 %all-gather = bf16[1,1024,256]{2,1,0:T(8,128)(2,1)S(1)} all-gather(bf16[1,16,256]{2,1,0:T(8,128)(2,1)S(1)} %copy.54), channel_id=2, replica_groups=mesh['ctx'=8,'tp'=16,'section'=8] {'ctx','section'}, dimensions={1}, use_global_device_ids=true | all-gather | bytes 532480 | tf_op jit(solution)/shard_map/all_gather | solution.py:100
  272.0 10.3 %while.31 = (s32[]{:T(128)}, f32[2,1,4,128]{3,2,0,1:T(4,128)S(1)}, f32[2,1,4,128]{3,2,0,1:T(4,128)S(1)}, f32[2,1,4,128,128]{3,4,2,0,1:T(8,128)}, bf16[2,512,1,2,...) while((s32[]{:T(128)}, f32[2,1,4,128]{3,2,0,1:T(4,128)S(1)}, ...), condition=%wide.region_10.11_spmd.clone, body=%wide.region_7.10_spmd.clone.sunk | while | flops 273029120 | bytes 10027137 | solution.py:122
  282.3 12.5 %reshape.180 = bf16[2,16,512,1,2,128]{5,4,2,1,0,3:T(2,128)(2,1)} reshape(bf16[2,8192,256]{2,1,0:T(8,128)(2,1)} %all-gather.3.cloned.1.call-done) | data formatting | bytes 16777216 | tf_op jit(solution)/shard_map/reshape | solution.py:60
  294.9 14.7 %copy.64 = bf16[2,16,512,1,2,128]{2,1,5,4,0,3:T(8,128)(2,1)} copy(bf16[2,16,512,1,2,128]{5,4,2,1,0,3:T(2,128)(2,1)} %reshape.180) | data formatting | bytes 16777216 | tf_op jit(solution)/shard_map/reshape | solution.py:60
  309.6 14.6 %copy.50 = bf16[16,2,512,1,2,128]{5,2,1,4,3,0:T(8,128)(2,1)} copy(bf16[16,2,512,1,2,128]{2,0,5,4,1,3:T(8,128)(2,1)} %bitcast.142) | data formatting | bytes 16777216
  324.3 77.3 %while.30 = (s32[]{:T(128)}, f32[2,1,4,128]{3,2,0,1:T(4,128)S(1)}, f32[2,1,4,128]{3,2,0,1:T(4,128)S(1)}, f32[2,1,4,128,128]{4,3,2,0,1:T(8,128)S(1)}, s32[16]{0:T...) while((s32[]{:T(128)}, f32[2,1,4,128]{3,2,0,1:T(4,128)S(1)}, ...), condition=%wide.region_6.7_spmd.clone, body=%wide.region_1.6_spmd.clone.sunk | while | flops 275714688 | bytes 9910583 | solution.py:87
  325.6 3.5 conditional.3
  330.4 3.5 conditional.3
  335.2 3.5 conditional.3
  340.1 3.5 conditional.3
  344.9 3.5 conditional.3
  349.7 3.5 conditional.3
  354.5 3.5 conditional.3
  359.4 3.5 conditional.3
  364.2 3.5 conditional.3
  369.0 3.5 conditional.3
  373.9 3.5 conditional.3
  378.7 3.5 conditional.3
  383.5 3.5 conditional.3
  388.3 3.5 conditional.3
  393.2 3.5 conditional.3
  398.0 3.5 conditional.3
  (294 shorter events, 85.2 us)
Async XLA Ops:
  6.5 1.2 copy-start
  6.5 275.8 %all-gather.3.cloned.1.call-start = ((), (), s32[]{:S(2)}) async-start(), calls=%async_computation.1 | async-start | bytes 8519680 | tf_op jit(solution)/shard_map/all_gather | solution.py:56
  11.1 46.3 %all-to-all-start = ((bf16[16,2,128]{2,1,0:T(2,128)(2,1)}), bf16[16,2,128]{2,1,0:T(2,128)(2,1)S(1)}, u32[]{:S(2)}, u32[]{:S(2)}) async-start(bf16[16,2,128]{2,1,0:T(2,128)(2,1)} %reshape.182), calls=%async_computation | async-start | bytes 16384 | tf_op jit(solution)/shard_map/all_to_all | solution.py:92
  273.2 0.7 copy-start.1
  278.2 0.7 copy-start.1
  309.6 14.7 %copy-start.3 = (s32[2]{0:T(128)S(1)}, s32[2]{0:T(128)}, u32[]{:S(2)}) copy-start(s32[2]{0:T(128)} %param.15) | copy-start | bytes 28
  324.3 77.5 %copy-start.2 = (f32[2,1,4,128,128]{3,4,2,0,1:T(8,128)S(1)}, f32[2,1,4,128,128]{3,4,2,0,1:T(8,128)}, u32[]{:S(2)}) copy-start(f32[2,1,4,128,128]{3,4,2,0,1:T(8,128)} %get-tuple-element.169) | copy-start | bytes 1572868
Sparse Core Ops, SparseCore 0:
  10.1 205.8 all-gather.2
where the time goes:
time: 412 us; the launch traced here: 410 us
  blocking collectives  214 us (52%)
  local copies, waits for them, and re-layouts  79.6 us (19%)
  matrix products  27.9 us (7%)
  starting transfers between devices  23.1 us (6%)
  other arithmetic  19.5 us (5%)
  waiting for transfers between devices  19.2 us (5%)
  between operations  14.2 us (3%)
  loops' own time  12.4 us (3%)
    all_gather x1, blocking collectives, per_device(): kv_piece = lax.all_gather(image_own, ('ctx', 'section'), axis=0, tiled=True)  214 us
    reshape x2, local copies, waits for them, and re-layouts, per_device(): kv_piece.reshape(2, row_count // block_rows, block_rows, kv_local, 2, HEA...  27.2 us
    all_to_all x1, starting transfers between devices, per_device(): lax.all_to_all(copies.reshape(image_rows, tp_count * kv_cols), 'tp', spli...  23.1 us
    dot_general x18, matrix products, fold_block(): jnp.einsum(value_form, weights.astype(jnp.bfloat16), value_matrix, prefer...  19.8 us
    all_to_all x1, waiting for transfers between devices, per_device(): lax.all_to_all(copies.reshape(image_rows, tp_count * kv_cols), 'tp', spli...  19.2 us
    unnamed x12, local copies, waits for them, and re-layouts  18.3 us
    squeeze x16, local copies, waits for them, and re-layouts, per_device(): lax.scan(self_one_block, carry_state, (jnp.arange(row_count // block_rows...  17.3 us
    another operation x1, loops' own time, per_device(): lax.scan(self_one_block, carry_state, (jnp.arange(row_count // block_rows...  11.3 us
  transfers between devices with their start and end apart: 2, of which 1 were waited for; matrix products, arithmetic and copies ran while one was open for 4% of the time, Pallas kernels for 0%

commit v1 on v0

v1 whole, which is shorter than its diff:
```python
import functools
import math

import jax
import jax.numpy as jnp
from jax import lax
from jax.experimental import pallas as pl
from jax.experimental.pallas import tpu as pltpu
from jax.sharding import PartitionSpec as P

HQ = 64
KVH = 8
D = 128
B = 128
ZL = 8
ZR = 32
Y = 4
X = 4
ROWS = 512
CHUNK = 512
NEG = -1e30
SCALE = math.log2(math.e) / math.sqrt(D)
MESH = pl.DeviceIdType.MESH


def attention_kernel(
    q_ref, kv_ref, img_ref, gate_ref, len_ref, out_ref,
    kv_all, rows, img_all, qt, acc, best, total,
    kv_recv, z_send, up_send, down_send, mate_send,
    row_recv, row_right, row_left, x_recv, x_send, img_recv, img_send, local,
):
    ctx = lax.axis_index("ctx")
    tp = lax.axis_index("tp")
    z = lax.axis_index("section")
    y, c = ctx // 2, ctx % 2
    x, zh = tp // 4, tp % 4
    zp = zh * ZL + z
    head = tp // 2
    rank = ctx * ZL + z

    def z_ring(step):
        at = (zp + step + ZR) % ZR
        return {"tp": x * 4 + at // ZL, "section": at % ZL}

    right, left = z_ring(1), z_ring(-1)
    up = {"ctx": ((y + 1) % Y) * 2 + c}
    down = {"ctx": ((y + Y - 1) % Y) * 2 + c}
    mate = {"ctx": y * 2 + (1 - c)}

    def x_peer(step):
        return {"tp": ((x + step) % X) * 4 + zh}

    def span(block):
        return pl.ds(pl.multiple_of(block * B, B), B)

    def piece(block, s):
        return kv_all.at[s, span(block), :]

    def remote(src, dst, send_sem, recv_sem, to):
        return pltpu.make_async_remote_copy(
            src_ref=src, dst_ref=dst, send_sem=send_sem, recv_sem=recv_sem,
            device_id=to, device_id_type=MESH,
        )

    def move(block, s, send_sem, to):
        return remote(piece(block, s), piece(block, s), send_sem, kv_recv.at[block * 2 + s], to)

    own_cols = pl.ds(pl.multiple_of(head * 2 * D, 2 * D), 2 * D)
    own_kv = [
        pltpu.make_async_copy(kv_ref.at[s, :, own_cols], piece(rank, s), local.at[s]) for s in (0, 1)
    ]
    own_row = pltpu.make_async_copy(img_ref, rows.at[zp], local.at[2])
    for cp in own_kv:
        cp.start()
    own_row.start()

    barrier = pltpu.get_barrier_semaphore()
    peers = (right, left, up, down, mate, x_peer(1), x_peer(2), x_peer(3))
    for peer in peers:
        pl.semaphore_signal(barrier, inc=1, device_id=peer, device_id_type=MESH)
    pl.semaphore_wait(barrier, len(peers))

    def row_move(at, send_sem, to):
        return remote(rows.at[at], rows.at[at], send_sem, row_recv.at[at], to)

    def row_step(j):
        from_left = (zp - 1 - j + 2 * ZR) % ZR
        from_right = (zp + 1 + j) % ZR
        row_move(from_left, row_right.at[0], right).wait_recv()

        @pl.when(j < 15)
        def _():
            row_move(from_left, row_right.at[j + 1], right).start()
            row_move(from_right, row_left.at[0], left).wait_recv()

        @pl.when(j < 14)
        def _():
            row_move(from_right, row_left.at[j + 1], left).start()

    def mate_slot(row, at, s):
        return mate_send.at[(row * ZL + at) * 2 + s]

    def block_of(row, at):
        return (row * 2 + c) * ZL + at

    def spread(at, s):
        block = block_of(y, at)
        move(block, s, up_send.at[at * 2 + s], up).start()
        move(block, s, down_send.at[at * 2 + s], down).start()
        move(block, s, mate_slot(y, at, s), mate).start()

    def z_step(d, s):
        @pl.when(z - d >= 0)
        def _():
            at = z - d
            move(block_of(y, at), s, z_send.at[at * 2 + s], right).wait_recv()

            @pl.when(z < ZL - 1)
            def _():
                move(block_of(y, at), s, z_send.at[at * 2 + s], right).start()

            spread(at, s)

        @pl.when(z + d < ZL)
        def _():
            at = z + d
            move(block_of(y, at), s, z_send.at[at * 2 + s], left).wait_recv()

            @pl.when(z > 0)
            def _():
                move(block_of(y, at), s, z_send.at[at * 2 + s], left).start()

            spread(at, s)

    below, above, across = (y + Y - 1) % Y, (y + 1) % Y, (y + 2) % Y

    def y_item(at, s):
        block = block_of(below, at)
        move(block, s, up_send.at[0], up).wait_recv()
        if s == 0:
            move(block, s, up_send.at[2 * ZL + at], up).start()
        move(block, s, mate_slot(below, at, s), mate).start()
        block = block_of(above, at)
        move(block, s, down_send.at[0], down).wait_recv()
        if s == 1:
            move(block, s, down_send.at[2 * ZL + at], down).start()
        move(block, s, mate_slot(above, at, s), mate).start()

    def across_item(at, s):
        block = block_of(across, at)
        move(block, s, up_send.at[0], up).wait_recv()
        move(block, s, mate_slot(across, at, s), mate).start()

    def both_sides(d, item):
        for s in (0, 1):
            @pl.when(z - d >= 0)
            def _():
                item(z - d, s)

            @pl.when(z + d < ZL)
            def _():
                item(z + d, s)

    own_row.wait()
    row_move(zp, row_right.at[0], right).start()
    row_move(zp, row_left.at[0], left).start()
    for s in (0, 1):
        own_kv[s].wait()

        @pl.when(z < ZL - 1)
        def _():
            move(rank, s, z_send.at[16 + s], right).start()

        @pl.when(z > 0)
        def _():
            move(rank, s, z_send.at[18 + s], left).start()

        spread(z, s)

    for s in (0, 1):
        for h in range(4):
            qt[s, :, h * B : (h + 1) * B] = q_ref[s, :, h * D : (h + 1) * D].T

    def gather_steps(d):
        for s in (0, 1):
            row_step(2 * (d - 1) + s)
            z_step(d, s)

    @pl.loop(0, 3)
    def _(t):
        gather_steps(2 * t + 1)
        gather_steps(2 * t + 2)

        @pl.when(t == 0)
        def _():
            y_item(z, 0)
            y_item(z, 1)

        @pl.when(t > 0)
        def _():
            both_sides(t, y_item)

    gather_steps(7)
    row_step(14)
    row_step(15)

    def head_rows(h):
        return rows.at[:, h]

    x_moves = []
    for step in (1, 2, 3):
        peer_head = 2 * ((x + step) % X) + zh // 2
        x_moves.append(
            remote(head_rows(peer_head), img_all.at[ctx, x], x_send.at[step], x_recv.at[x], x_peer(step))
        )
    own_head = pltpu.make_async_copy(head_rows(head), img_all.at[ctx, x], local.at[3])
    for cp in x_moves:
        cp.start()
    own_head.start()

    def img_move(at, send_sem, to):
        return remote(img_all.at[at], img_all.at[at], send_sem, img_recv.at[at], to)

    both_sides(3, y_item)
    own_head.wait()
    for step in (1, 2, 3):
        src = (x + X - step) % X
        remote(head_rows(head), img_all.at[ctx, src], x_send.at[0], x_recv.at[src], x_peer(1)).wait_recv()
    img_sends = [img_move(ctx, img_send.at[0], up), img_move(ctx, img_send.at[1], down), img_move(ctx, img_send.at[2], mate)]
    for cp in img_sends:
        cp.start()

    @pl.loop(4, ZL)
    def _(d):
        both_sides(d, y_item)

        @pl.when(d == 4)
        def _():
            across_item(z, 0)
            across_item(z, 1)

        @pl.when(d > 4)
        def _():
            both_sides(d - 4, across_item)

    at = below * 2 + c
    img_move(at, img_send.at[0], up).wait_recv()
    more = [img_move(at, img_send.at[3], up), img_move(at, img_send.at[4], mate)]
    for cp in more:
        cp.start()
    img_sends += more
    for slot, row in ((5, above), (6, across)):
        at = row * 2 + c
        img_move(at, img_send.at[0], up).wait_recv()
        cp = img_move(at, img_send.at[slot], mate)
        cp.start()
        img_sends.append(cp)

    @pl.loop(4, ZL)
    def _(d):
        both_sides(d, across_item)

    @pl.loop(0, Y)
    def _(row):
        img_move(row * 2 + 1 - c, img_send.at[0], mate).wait_recv()

        @pl.loop(0, ZL)
        def _(at):
            for s in (0, 1):
                move((row * 2 + 1 - c) * ZL + at, s, up_send.at[0], mate).wait_recv()

    key_iota = lax.broadcasted_iota(jnp.int32, (CHUNK, ROWS), 0)
    query_pos = rank * B + lax.broadcasted_iota(jnp.int32, (1, ROWS), 1) % B

    def start_rows():
        best[...] = jnp.full_like(best, NEG)
        total[...] = jnp.zeros_like(total)
        acc[...] = jnp.zeros_like(acc)

    def fold(s, keys, values, limit):
        scores = jnp.dot(keys, qt[s], preferred_element_type=jnp.float32) * SCALE
        if limit is not None:
            scores = jnp.where(key_iota < limit, scores, NEG)
        old = best[...]
        new = jnp.maximum(old, jnp.max(scores, axis=0, keepdims=True))
        weights = jnp.exp2(scores - new)
        shrink = jnp.exp2(old - new)
        best[...] = new
        total[...] = total[...] * shrink + jnp.sum(weights, axis=0, keepdims=True)
        acc[...] = acc[...] * shrink + lax.dot_general(
            values, weights.astype(jnp.bfloat16), (((0,), (0,)), ((), ())),
            preferred_element_type=jnp.float32,
        )

    gates = jnp.tanh(gate_ref[...])
    gate_row = jnp.concatenate(
        [jnp.broadcast_to(gates[:, h : h + 1], (1, B)) for h in range(4)], axis=1
    )
    for s in (0, 1):
        start_rows()
        limit = jnp.minimum(query_pos + 1, len_ref[s])

        @pl.loop(0, rank // (CHUNK // B) + 1)
        def _(n):
            first = pl.multiple_of(n * CHUNK, CHUNK)
            fold(
                s, kv_all[s, pl.ds(first, CHUNK), :D], kv_all[s, pl.ds(first, CHUNK), D:],
                limit - first,
            )

        self_out = acc[...] / total[...]
        start_rows()

        @pl.loop(0, 2)
        def _(n):
            pairs = img_all[pl.ds(4 * n, 4)]
            fold(s, pairs[:, :, :, 0].reshape(CHUNK, D), pairs[:, :, :, 1].reshape(CHUNK, D), None)

        attended = self_out + gate_row * (acc[...] / total[...])
        for h in range(4):
            out_ref[s, :, h * D : (h + 1) * D] = attended[:, h * B : (h + 1) * B].T.astype(jnp.bfloat16)

    for cp in x_moves + img_sends:
        cp.wait_send()

    @pl.loop(0, 16)
    def _(j):
        row_move(zp, row_right.at[j], right).wait_send()

    @pl.loop(0, 15)
    def _(j):
        row_move(zp, row_left.at[j], left).wait_send()

    for s in (0, 1):
        @pl.when(z < ZL - 1)
        def _():
            move(rank, s, z_send.at[16 + s], right).wait_send()

        @pl.when(z > 0)
        def _():
            move(rank, s, z_send.at[18 + s], left).wait_send()

    @pl.loop(0, ZL)
    def _(at):
        @pl.when(((at < z) & (z < ZL - 1)) | ((at > z) & (z > 0)))
        def _():
            for s in (0, 1):
                move(rank, s, z_send.at[at * 2 + s], right).wait_send()

    @pl.loop(0, 3 * ZL)
    def _(j):
        move(rank, 0, up_send.at[j], up).wait_send()
        move(rank, 0, down_send.at[j], down).wait_send()

    @pl.loop(0, 2 * Y * ZL)
    def _(j):
        move(rank, 0, mate_send.at[j], mate).wait_send()


def per_device(queries, self_kv, image_kv, cross_gate, lengths):
    vmem = pl.BlockSpec(memory_space=pltpu.VMEM)
    dma = pltpu.SemaphoreType.DMA
    return pl.pallas_call(
        attention_kernel,
        out_shape=jax.ShapeDtypeStruct(queries.shape, queries.dtype),
        in_specs=[
            vmem,
            pl.BlockSpec(memory_space=pl.ANY),
            vmem,
            vmem,
            pl.BlockSpec(memory_space=pltpu.SMEM),
        ],
        out_specs=vmem,
        scratch_shapes=[
            pltpu.VMEM((2, 64 * B, 2 * D), jnp.bfloat16),
            pltpu.VMEM((ZR, KVH, 2, D), jnp.bfloat16),
            pltpu.VMEM((8, X, ZR, 2, D), jnp.bfloat16),
            pltpu.VMEM((2, D, ROWS), jnp.bfloat16),
            pltpu.VMEM((D, ROWS), jnp.float32),
            pltpu.VMEM((1, ROWS), jnp.float32),
            pltpu.VMEM((1, ROWS), jnp.float32),
            dma((128,)),
            dma((20,)),
            dma((24,)),
            dma((24,)),
            dma((64,)),
            dma((ZR,)),
            dma((16,)),
            dma((15,)),
            dma((X,)),
            dma((X,)),
            dma((8,)),
            dma((7,)),
            dma((4,)),
        ],
        compiler_params=pltpu.CompilerParams(
            collective_id=0, has_side_effects=True, vmem_limit_bytes=56 * 1024 * 1024
        ),
    )(queries, self_kv, image_kv.reshape(KVH, 2, D), cross_gate.reshape(1, 4), lengths)


def solution(mesh):
    placed = (
        P(None, ("ctx", "section"), "tp"),
        P(None, ("ctx", "section"), None),
        P(("ctx", "tp", "section"), None),
        P("tp"),
        P(),
    )
    return jax.shard_map(
        per_device,
        mesh=mesh,
        in_specs=placed,
        out_specs=P(None, ("ctx", "section"), "tp"),
        check_vma=False,
    )
```

time: 412 us -> 111 us (0.27)
  the two profiles are of different devices: /device:TPU:249 before, /device:TPU:25 now
where the time goes in v1:
time: 111 us
  Pallas kernels  108 us (97%)
  local copies, waits for them, and re-layouts  1.67 us (2%)
  other arithmetic  1.32 us (1%)
    pallas_call x1, Pallas kernels, per_device(): pl.pallas_call(attention_kernel, out_shape=jax.ShapeDtypeStruct(queries.s...  108 us

profile of v1, /device:TPU:25, one launch (start us, length us, event | category | flops | bytes accessed | tf_op | source)
XLA Modules:
  0.0 111.0 jit_solution(7114219110536740134)
XLA Ops:
  0.0 1.3 %reduce = bf16[2048]{0:T(1024)(128)(2,1)} reduce(bf16[1,2048]{1,0:T(2,128)(2,1)} %param.7, bf16[]{:T(256)} %constant.2), dimensions={0}, to_apply=%param.7.reduce_sub_computation | reduce | bytes 8194 | tf_op args[2]
  1.3 108.0 %shard_map.55 = bf16[2,128,512]{2,1,0:T(8,128)(2,1)} custom-call(bf16[2,128,512]{2,1,0:T(8,128)(2,1)} %q_ref.1, bf16[2,128,2048]{2,1,0:T(8,128)(2,1)} %kv_ref.1, bf16[8,2,128]{2,1,0:T(2,128)(2,1)} %bitcast.2, f32[1,4]{1,0:T(1,128)} %bitcast.3, s32[2]{0:T(128)} %len_ref.1), custom_call_target="tpu_custom_call" | custom-call | tf_op jit(solution)/shard_map/pallas_call | solution.py:363
  109.3 1.7 %copy.7 = bf16[2,128,512]{2,1,0:T(8,128)(2,1)} copy(bf16[2,128,512]{2,1,0:T(8,128)(2,1)} %shard_map.55) | data formatting | bytes 524288

commit v2 on v1

v2 whole, which is shorter than its diff:
```python
import functools
import math

import jax
import jax.numpy as jnp
from jax import lax
from jax.experimental import pallas as pl
from jax.experimental.pallas import tpu as pltpu
from jax.sharding import PartitionSpec as P

HQ = 64
KVH = 8
D = 128
B = 128
ZL = 8
ZR = 32
Y = 4
X = 4
ROWS = 512
CHUNK = 512
EARLY = 20
MID = 2
NEG = -1e30
SCALE = math.log2(math.e) / math.sqrt(D)
MESH = pl.DeviceIdType.MESH


def attention_kernel(
    q_ref, kv_ref, img_ref, gate_ref, len_ref, out_ref,
    kv_all, xrows, img_all, qt, acc, best, total, self_out, limits,
    kv_recv, z_send, up_send, down_send, mate_send,
    x_recv, x_send, row_recv, row_send, img_recv, img_send, local, token,
):
    ctx = lax.axis_index("ctx")
    tp = lax.axis_index("tp")
    z = lax.axis_index("section")
    y, c = ctx // 2, ctx % 2
    x, zh = tp // 4, tp % 4
    zp = zh * ZL + z
    head = tp // 2
    rank = ctx * ZL + z

    def z_line(at):
        return {"tp": x * 4 + at // ZL, "section": at % ZL}

    right, left = z_line(jnp.minimum(zp + 1, ZR - 1)), z_line(jnp.maximum(zp - 1, 0))
    up = {"ctx": ((y + 1) % Y) * 2 + c}
    down = {"ctx": ((y + Y - 1) % Y) * 2 + c}
    mate = {"ctx": y * 2 + (1 - c)}

    def x_peer(step):
        return {"tp": ((x + step) % X) * 4 + zh}

    def span(block):
        return pl.ds(pl.multiple_of(block * B, B), B)

    def piece(block, s):
        return kv_all.at[s, span(block), :]

    def remote(src, dst, send_sem, recv_sem, to):
        return pltpu.make_async_remote_copy(
            src_ref=src, dst_ref=dst, send_sem=send_sem, recv_sem=recv_sem,
            device_id=to, device_id_type=MESH,
        )

    def move(block, s, send_sem, to):
        return remote(piece(block, s), piece(block, s), send_sem, kv_recv.at[block * 2 + s], to)

    own_cols = pl.ds(pl.multiple_of(head * 2 * D, 2 * D), 2 * D)
    own_kv = [
        pltpu.make_async_copy(kv_ref.at[s, :, own_cols], piece(rank, s), local.at[s]) for s in (0, 1)
    ]
    for cp in own_kv:
        cp.start()

    barrier = pltpu.get_barrier_semaphore()
    peers = (up, down, mate, x_peer(1), x_peer(2), x_peer(3))
    for peer in peers:
        pl.semaphore_signal(barrier, inc=1, device_id=peer, device_id_type=MESH)

    def greet(at):
        pl.semaphore_signal(barrier, inc=1, device_id=z_line(at), device_id_type=MESH)

    @pl.when(zp > 0)
    def _():
        greet(zp - 1)

    @pl.when((zp >= EARLY - 1) & (zp < ZR - 1))
    def _():
        greet(zp + 1)

    @pl.loop(zp + 1, EARLY)
    def _(at):
        greet(at)

    @pl.when(zp < ZL)
    def _():
        @pl.loop(EARLY, ZR)
        def _(at):
            greet(at)

    lower = jnp.where(zp < EARLY, zp, ZL)
    below_is_extra = jnp.where(zp < EARLY, 0, 1)
    above_is_there = jnp.where(zp < ZR - 1, 1, 0)
    pl.semaphore_wait(barrier, len(peers) + lower + below_is_extra + above_is_there)

    def x_move(to, src, step):
        return remote(img_ref.at[to], xrows.at[src], x_send.at[step], x_recv.at[src], x_peer(step))

    def row_move(to, src):
        return remote(
            xrows.at[:, to // 16], img_all.at[ctx, src], row_send.at[to], row_recv.at[src], z_line(to)
        )

    own_x = pltpu.make_async_copy(img_ref.at[x], xrows.at[x], local.at[2])
    own_z = pltpu.make_async_copy(xrows.at[:, zp // 16], img_all.at[ctx, zp], local.at[3])

    def rows_down():
        for step in (1, 2, 3):
            src = (x + X - step) % X
            x_move(x, src, step).wait_recv()
        own_x.wait()
        own_z.start()

        @pl.loop(0, lower)
        def _(at):
            row_move(at, zp).start()

        @pl.when(zp == EARLY - 1)
        def _():
            pl.semaphore_signal(token, inc=1, device_id=right, device_id_type=MESH)

    def rows_down_late():
        @pl.when(zp >= EARLY)
        def _():
            pl.semaphore_wait(token, 1)

            @pl.when(zp < ZR - 1)
            def _():
                pl.semaphore_signal(token, inc=1, device_id=right, device_id_type=MESH)

            @pl.loop(ZL, zp)
            def _(at):
                row_move(at, zp).start()

    def rows_back(first, last):
        @pl.loop(first, last)
        def _(at):
            row_move(at, at).wait_recv()
            row_move(at, zp).start()

    own_x.start()
    for step in (1, 2, 3):
        x_move((x + step) % X, x, step).start()

    def mate_slot(row, at, s):
        return mate_send.at[(row * ZL + at) * 2 + s]

    def block_of(row, at):
        return (row * 2 + c) * ZL + at

    def spread(at, s):
        block = block_of(y, at)
        move(block, s, up_send.at[at * 2 + s], up).start()
        move(block, s, down_send.at[at * 2 + s], down).start()
        move(block, s, mate_slot(y, at, s), mate).start()

    def z_step(d, s):
        @pl.when(z - d >= 0)
        def _():
            at = z - d
            move(block_of(y, at), s, z_send.at[at * 2 + s], right).wait_recv()

            @pl.when(z < ZL - 1)
            def _():
                move(block_of(y, at), s, z_send.at[at * 2 + s], right).start()

            spread(at, s)

        @pl.when(z + d < ZL)
        def _():
            at = z + d
            move(block_of(y, at), s, z_send.at[at * 2 + s], left).wait_recv()

            @pl.when(z > 0)
            def _():
                move(block_of(y, at), s, z_send.at[at * 2 + s], left).start()

            spread(at, s)

    below, above, across = (y + Y - 1) % Y, (y + 1) % Y, (y + 2) % Y

    def y_item(at, s):
        block = block_of(below, at)
        move(block, s, up_send.at[0], up).wait_recv()
        if s == 0:
            move(block, s, up_send.at[2 * ZL + at], up).start()
        move(block, s, mate_slot(below, at, s), mate).start()
        block = block_of(above, at)
        move(block, s, down_send.at[0], down).wait_recv()
        if s == 1:
            move(block, s, down_send.at[2 * ZL + at], down).start()
        move(block, s, mate_slot(above, at, s), mate).start()

    def across_item(at, s):
        block = block_of(across, at)
        move(block, s, up_send.at[0], up).wait_recv()
        move(block, s, mate_slot(across, at, s), mate).start()

    def both_sides(d, item):
        for s in (0, 1):
            @pl.when(z - d >= 0)
            def _():
                item(z - d, s)

            @pl.when(z + d < ZL)
            def _():
                item(z + d, s)

    for s in (0, 1):
        own_kv[s].wait()

        @pl.when(z < ZL - 1)
        def _():
            move(rank, s, z_send.at[16 + s], right).start()

        @pl.when(z > 0)
        def _():
            move(rank, s, z_send.at[18 + s], left).start()

        spread(z, s)

    for s in (0, 1):
        for h in range(4):
            qt[s, :, h * B : (h + 1) * B] = q_ref[s, :, h * D : (h + 1) * D].T

    key_iota = lax.broadcasted_iota(jnp.int32, (CHUNK, ROWS), 0)
    query_pos = rank * B + lax.broadcasted_iota(jnp.int32, (1, ROWS), 1) % B
    for s in (0, 1):
        limits[s] = jnp.minimum(query_pos + 1, len_ref[s])

    def start_rows():
        best[...] = jnp.full_like(best, NEG)
        total[...] = jnp.zeros_like(total)
        acc[...] = jnp.zeros_like(acc)

    def fold(s, keys, values, limit):
        scores = jnp.dot(keys, qt[s], preferred_element_type=jnp.float32) * SCALE
        if limit is not None:
            scores = jnp.where(key_iota < limit, scores, NEG)
        old = best[s]
        new = jnp.maximum(old, jnp.max(scores, axis=0, keepdims=True))
        weights = jnp.exp2(scores - new)
        shrink = jnp.exp2(old - new)
        best[s] = new
        total[s] = total[s] * shrink + jnp.sum(weights, axis=0, keepdims=True)
        acc[s] = acc[s] * shrink + lax.dot_general(
            values, weights.astype(jnp.bfloat16), (((0,), (0,)), ((), ())),
            preferred_element_type=jnp.float32,
        )

    near = z // 4
    far = 1 - near

    def fold_half(row, core, half):
        block = (row * 2 + core) * ZL + half * 4

        @pl.when(core != c)
        def _():
            @pl.loop(0, 4)
            def _(k):
                for s in (0, 1):
                    move(block + k, s, up_send.at[0], mate).wait_recv()

        @pl.when(block // 4 <= rank // 4)
        def _():
            first = pl.multiple_of(block * B, CHUNK)

            @pl.loop(0, 2)
            def _(s):
                fold(
                    s, kv_all[s, pl.ds(first, CHUNK), :D], kv_all[s, pl.ds(first, CHUNK), D:],
                    limits[s] - first,
                )

    def gather_steps(d):
        z_step(d, 0)
        z_step(d, 1)

    start_rows()
    rows_down()
    gather_steps(1)
    gather_steps(2)
    rows_down_late()
    y_item(z, 0)
    y_item(z, 1)
    gather_steps(3)

    @pl.loop(0, 2)
    def _(t):
        gather_steps(4 + 2 * t)
        fold_half(y, (c + t) % 2, near)
        both_sides(1 + t, y_item)
        gather_steps(5 + 2 * t)

    run_end = (zh + 1) * ZL
    rows_back(zp + 1, run_end)
    both_sides(3, y_item)

    def neighbour_row(t):
        return (y + 3 + 2 * (t // 2)) % Y

    @pl.loop(0, 2)
    def _(t):
        fold_half(y, (c + t) % 2, far)

    @pl.loop(0, MID)
    def _(t):
        both_sides(4 + t, y_item)

        @pl.when(t == 0)
        def _():
            across_item(z, 0)
            across_item(z, 1)

        @pl.when(t > 0)
        def _():
            both_sides(t, across_item)

        fold_half(neighbour_row(t), (c + t) % 2, near)

    rows_back(run_end, ZR)

    @pl.loop(MID, 4)
    def _(t):
        both_sides(4 + t, y_item)

        @pl.when(t == 0)
        def _():
            across_item(z, 0)
            across_item(z, 1)

        @pl.when(t > 0)
        def _():
            both_sides(t, across_item)

        fold_half(neighbour_row(t), (c + t) % 2, near)

    @pl.loop(0, zp)
    def _(at):
        row_move(zp, at).wait_recv()

    own_z.wait()

    def img_move(at, send_sem, to):
        return remote(img_all.at[at], img_all.at[at], send_sem, img_recv.at[at], to)

    img_sends = [img_move(ctx, img_send.at[0], up), img_move(ctx, img_send.at[1], down), img_move(ctx, img_send.at[2], mate)]
    for cp in img_sends:
        cp.start()

    @pl.loop(0, 4)
    def _(t):
        both_sides(4 + t, across_item)
        fold_half(neighbour_row(t), (c + t) % 2, far)

    at = below * 2 + c
    img_move(at, img_send.at[0], up).wait_recv()
    more = [img_move(at, img_send.at[3], up), img_move(at, img_send.at[4], mate)]
    for cp in more:
        cp.start()
    img_sends += more
    at = above * 2 + c
    img_move(at, img_send.at[0], up).wait_recv()
    cp = img_move(at, img_send.at[5], mate)
    cp.start()
    img_sends.append(cp)

    @pl.loop(0, 4)
    def _(t):
        fold_half(across, (c + t) % 2, (near + t // 2) % 2)

    at = across * 2 + c
    img_move(at, img_send.at[0], up).wait_recv()
    cp = img_move(at, img_send.at[6], mate)
    cp.start()
    img_sends.append(cp)

    for s in (0, 1):
        self_out[s] = acc[s] / total[s]
    start_rows()

    @pl.loop(0, Y)
    def _(row):
        img_move(row * 2 + 1 - c, img_send.at[0], mate).wait_recv()

    gates = jnp.tanh(gate_ref[...])
    gate_row = jnp.concatenate(
        [jnp.broadcast_to(gates[:, h : h + 1], (1, B)) for h in range(4)], axis=1
    )

    @pl.loop(0, 2)
    def _(n):
        pairs = img_all[pl.ds(4 * n, 4)]
        keys, values = pairs[:, :, :, 0].reshape(CHUNK, D), pairs[:, :, :, 1].reshape(CHUNK, D)
        for s in (0, 1):
            fold(s, keys, values, None)

    for s in (0, 1):
        attended = self_out[s] + gate_row * (acc[s] / total[s])
        for h in range(4):
            out_ref[s, :, h * D : (h + 1) * D] = attended[:, h * B : (h + 1) * B].T.astype(jnp.bfloat16)

    for cp in img_sends:
        cp.wait_send()
    for step in (1, 2, 3):
        x_move(x, x, step).wait_send()

    @pl.loop(0, ZR)
    def _(to):
        @pl.when(to != zp)
        def _():
            row_move(to, zp).wait_send()

    for s in (0, 1):
        @pl.when(z < ZL - 1)
        def _():
            move(rank, s, z_send.at[16 + s], right).wait_send()

        @pl.when(z > 0)
        def _():
            move(rank, s, z_send.at[18 + s], left).wait_send()

    @pl.loop(0, ZL)
    def _(at):
        @pl.when(((at < z) & (z < ZL - 1)) | ((at > z) & (z > 0)))
        def _():
            for s in (0, 1):
                move(rank, s, z_send.at[at * 2 + s], right).wait_send()

    @pl.loop(0, 3 * ZL)
    def _(j):
        move(rank, 0, up_send.at[j], up).wait_send()
        move(rank, 0, down_send.at[j], down).wait_send()

    @pl.loop(0, 2 * Y * ZL)
    def _(j):
        move(rank, 0, mate_send.at[j], mate).wait_send()


def per_device(queries, self_kv, image_kv, cross_gate, lengths):
    vmem = pl.BlockSpec(memory_space=pltpu.VMEM)
    dma = pltpu.SemaphoreType.DMA
    return pl.pallas_call(
        attention_kernel,
        out_shape=jax.ShapeDtypeStruct(queries.shape, queries.dtype),
        in_specs=[
            vmem,
            pl.BlockSpec(memory_space=pl.ANY),
            vmem,
            vmem,
            pl.BlockSpec(memory_space=pltpu.SMEM),
        ],
        out_specs=vmem,
        scratch_shapes=[
            pltpu.VMEM((2, 64 * B, 2 * D), jnp.bfloat16),
            pltpu.VMEM((X, 2, 2, D), jnp.bfloat16),
            pltpu.VMEM((8, ZR, X, 2, D), jnp.bfloat16),
            pltpu.VMEM((2, D, ROWS), jnp.bfloat16),
            pltpu.VMEM((2, D, ROWS), jnp.float32),
            pltpu.VMEM((2, 1, ROWS), jnp.float32),
            pltpu.VMEM((2, 1, ROWS), jnp.float32),
            pltpu.VMEM((2, D, ROWS), jnp.float32),
            pltpu.VMEM((2, 1, ROWS), jnp.int32),
            dma((128,)),
            dma((20,)),
            dma((24,)),
            dma((24,)),
            dma((64,)),
            dma((X,)),
            dma((X,)),
            dma((ZR,)),
            dma((ZR,)),
            dma((8,)),
            dma((7,)),
            dma((4,)),
            pltpu.SemaphoreType.REGULAR,
        ],
        compiler_params=pltpu.CompilerParams(
            collective_id=0, has_side_effects=True, vmem_limit_bytes=56 * 1024 * 1024
        ),
    )(queries, self_kv, image_kv.reshape(X, 2, 2, D), cross_gate.reshape(1, 4), lengths)


def solution(mesh):
    placed = (
        P(None, ("ctx", "section"), "tp"),
        P(None, ("ctx", "section"), None),
        P(("ctx", "tp", "section"), None),
        P("tp"),
        P(),
    )
    return jax.shard_map(
        per_device,
        mesh=mesh,
        in_specs=placed,
        out_specs=P(None, ("ctx", "section"), "tp"),
        check_vma=False,
    )
```

time: 111 us -> 76.3 us (0.69)
  the two profiles are of different devices: /device:TPU:25 before, /device:TPU:1017 now
where the time goes in v2:
time: 76.3 us; the launch traced here: 76 us
  Pallas kernels  73.1 us (96%)
  local copies, waits for them, and re-layouts  1.67 us (2%)
  other arithmetic  1.32 us (2%)
    pallas_call x1, Pallas kernels, per_device(): pl.pallas_call(attention_kernel, out_shape=jax.ShapeDtypeStruct(queries.s...  73.1 us
    unnamed x1, local copies, waits for them, and re-layouts  1.67 us

profile of v2, /device:TPU:1017, one launch (start us, length us, event | category | flops | bytes accessed | tf_op | source)
XLA Modules:
  0.0 76.0 jit_solution(10117585607046842775)
XLA Ops:
  0.0 1.3 %reduce = bf16[2048]{0:T(1024)(128)(2,1)} reduce(bf16[1,2048]{1,0:T(2,128)(2,1)} %param.7, bf16[]{:T(256)} %constant.2), dimensions={0}, to_apply=%param.7.reduce_sub_computation | reduce | bytes 8194 | tf_op args[2]
  1.3 73.1 %shard_map.55 = bf16[2,128,512]{2,1,0:T(8,128)(2,1)} custom-call(bf16[2,128,512]{2,1,0:T(8,128)(2,1)} %q_ref.1, bf16[2,128,2048]{2,1,0:T(8,128)(2,1)} %kv_ref.1, bf16[4,2,2,128]{3,2,1,0:T(2,128)(2,1)} %bitcast.2, f32[1,4]{1,0:T(1,128)} %bitcast.3, s32[2]{0:T(128)} %len_ref.1), custom_call_target="tpu_custom_call" | custom-call | tf_op jit(solution)/shard_map/pallas_call | solution.py:454
  74.4 1.7 %copy.7 = bf16[2,128,512]{2,1,0:T(8,128)(2,1)} copy(bf16[2,128,512]{2,1,0:T(8,128)(2,1)} %shard_map.55) | data formatting | bytes 524288

commit v3 on v2

--- a/solution.py
+++ b/solution.py
@@ -19,7 +19,6 @@
 ROWS = 512
 CHUNK = 512
 EARLY = 20
-MID = 2
 NEG = -1e30
 SCALE = math.log2(math.e) / math.sqrt(D)
 MESH = pl.DeviceIdType.MESH
@@ -27,7 +26,7 @@
 
 def attention_kernel(
     q_ref, kv_ref, img_ref, gate_ref, len_ref, out_ref,
-    kv_all, xrows, img_all, qt, acc, best, total, self_out, limits,
+    kv_all, xrows, img_all, qt, acc, best, total, limits,
     kv_recv, z_send, up_send, down_send, mate_send,
     x_recv, x_send, row_recv, row_send, img_recv, img_send, local, token,
 ):
@@ -104,6 +103,10 @@
     above_is_there = jnp.where(zp < ZR - 1, 1, 0)
     pl.semaphore_wait(barrier, len(peers) + lower + below_is_extra + above_is_there)
 
+    @pl.when(zp == EARLY - 1)
+    def _():
+        pl.semaphore_signal(token, inc=1, device_id=right, device_id_type=MESH)
+
     def x_move(to, src, step):
         return remote(img_ref.at[to], xrows.at[src], x_send.at[step], x_recv.at[src], x_peer(step))
 
@@ -125,10 +128,6 @@
         @pl.loop(0, lower)
         def _(at):
             row_move(at, zp).start()
-
-        @pl.when(zp == EARLY - 1)
-        def _():
-            pl.semaphore_signal(token, inc=1, device_id=right, device_id_type=MESH)
 
     def rows_down_late():
         @pl.when(zp >= EARLY)
@@ -244,20 +243,22 @@
         total[...] = jnp.zeros_like(total)
         acc[...] = jnp.zeros_like(acc)
 
-    def fold(s, keys, values, limit):
-        scores = jnp.dot(keys, qt[s], preferred_element_type=jnp.float32) * SCALE
-        if limit is not None:
-            scores = jnp.where(key_iota < limit, scores, NEG)
-        old = best[s]
-        new = jnp.maximum(old, jnp.max(scores, axis=0, keepdims=True))
-        weights = jnp.exp2(scores - new)
-        shrink = jnp.exp2(old - new)
-        best[s] = new
-        total[s] = total[s] * shrink + jnp.sum(weights, axis=0, keepdims=True)
-        acc[s] = acc[s] * shrink + lax.dot_general(
-            values, weights.astype(jnp.bfloat16), (((0,), (0,)), ((), ())),
-            preferred_element_type=jnp.float32,
-        )
+    def fold(jobs, at):
+        scores = []
+        for s, (keys, _, limit) in enumerate(jobs):
+            raw = jnp.dot(keys, qt[s], preferred_element_type=jnp.float32) * SCALE
+            scores.append(raw if limit is None else jnp.where(key_iota < limit, raw, NEG))
+        for s, (_, values, _) in enumerate(jobs):
+            old = best[at + s]
+            new = jnp.maximum(old, jnp.max(scores[s], axis=0, keepdims=True))
+            weights = jnp.exp2(scores[s] - new)
+            shrink = jnp.exp2(old - new)
+            best[at + s] = new
+            total[at + s] = total[at + s] * shrink + jnp.sum(weights, axis=0, keepdims=True)
+            acc[at + s] = acc[at + s] * shrink + lax.dot_general(
+                values, weights.astype(jnp.bfloat16), (((0,), (0,)), ((), ())),
+                preferred_element_type=jnp.float32,
+            )
 
     near = z // 4
     far = 1 - near
@@ -276,12 +277,8 @@
         def _():
             first = pl.multiple_of(block * B, CHUNK)
 
-            @pl.loop(0, 2)
-            def _(s):
-                fold(
-                    s, kv_all[s, pl.ds(first, CHUNK), :D], kv_all[s, pl.ds(first, CHUNK), D:],
-                    limits[s] - first,
-                )
+            keys = pl.ds(first, CHUNK)
+            fold([(kv_all[s, keys, :D], kv_all[s, keys, D:], limits[s] - first) for s in (0, 1)], 0)
 
     def gather_steps(d):
         z_step(d, 0)
@@ -290,8 +287,8 @@
     start_rows()
     rows_down()
     gather_steps(1)
+    rows_down_late()
     gather_steps(2)
-    rows_down_late()
     y_item(z, 0)
     y_item(z, 1)
     gather_steps(3)
@@ -314,37 +311,21 @@
     def _(t):
         fold_half(y, (c + t) % 2, far)
 
-    @pl.loop(0, MID)
+    @pl.when(zp >= ZL)
+    def _():
+        rows_back(run_end, ZR)
+
+    @pl.loop(0, 4)
     def _(t):
         both_sides(4 + t, y_item)
-
-        @pl.when(t == 0)
-        def _():
-            across_item(z, 0)
-            across_item(z, 1)
-
-        @pl.when(t > 0)
-        def _():
-            both_sides(t, across_item)
-
         fold_half(neighbour_row(t), (c + t) % 2, near)
 
-    rows_back(run_end, ZR)
-
-    @pl.loop(MID, 4)
-    def _(t):
-        both_sides(4 + t, y_item)
-
-        @pl.when(t == 0)
-        def _():
-            across_item(z, 0)
-            across_item(z, 1)
-
-        @pl.when(t > 0)
-        def _():
-            both_sides(t, across_item)
-
-        fold_half(neighbour_row(t), (c + t) % 2, near)
+        @pl.when((t == 1) & (zp < ZL))
+        def _():
+            rows_back(run_end, ZR)
+
+    across_item(z, 0)
+    across_item(z, 1)
 
     @pl.loop(0, zp)
     def _(at):
@@ -359,36 +340,38 @@
     for cp in img_sends:
         cp.start()
 
+    at_below, at_above, at_across = below * 2 + c, above * 2 + c, across * 2 + c
+    img_relays = [
+        img_move(at_below, img_send.at[3], up), img_move(at_below, img_send.at[4], mate),
+        img_move(at_above, img_send.at[5], mate), img_move(at_across, img_send.at[6], mate),
+    ]
+
     @pl.loop(0, 4)
     def _(t):
-        both_sides(4 + t, across_item)
         fold_half(neighbour_row(t), (c + t) % 2, far)
 
-    at = below * 2 + c
-    img_move(at, img_send.at[0], up).wait_recv()
-    more = [img_move(at, img_send.at[3], up), img_move(at, img_send.at[4], mate)]
-    for cp in more:
-        cp.start()
-    img_sends += more
-    at = above * 2 + c
-    img_move(at, img_send.at[0], up).wait_recv()
-    cp = img_move(at, img_send.at[5], mate)
-    cp.start()
-    img_sends.append(cp)
-
-    @pl.loop(0, 4)
-    def _(t):
-        fold_half(across, (c + t) % 2, (near + t // 2) % 2)
-
-    at = across * 2 + c
-    img_move(at, img_send.at[0], up).wait_recv()
-    cp = img_move(at, img_send.at[6], mate)
-    cp.start()
-    img_sends.append(cp)
-
-    for s in (0, 1):
-        self_out[s] = acc[s] / total[s]
-    start_rows()
+        @pl.when(t < 3)
+        def _():
+            both_sides(1 + t, across_item)
+
+    img_move(at_below, img_send.at[0], up).wait_recv()
+    img_relays[0].start()
+    img_relays[1].start()
+    img_move(at_above, img_send.at[0], up).wait_recv()
+    img_relays[2].start()
+
+    @pl.loop(0, 2)
+    def _(t):
+        both_sides(4 + 2 * t, across_item)
+        fold_half(across, (c + t) % 2, near)
+        both_sides(5 + 2 * t, across_item)
+
+    img_move(at_across, img_send.at[0], up).wait_recv()
+    img_relays[3].start()
+
+    @pl.loop(0, 2)
+    def _(t):
+        fold_half(across, (c + t) % 2, far)
 
     @pl.loop(0, Y)
     def _(row):
@@ -403,15 +386,14 @@
     def _(n):
         pairs = img_all[pl.ds(4 * n, 4)]
         keys, values = pairs[:, :, :, 0].reshape(CHUNK, D), pairs[:, :, :, 1].reshape(CHUNK, D)
-        for s in (0, 1):
-            fold(s, keys, values, None)
+        fold([(keys, values, None)] * 2, 2)
 
     for s in (0, 1):
-        attended = self_out[s] + gate_row * (acc[s] / total[s])
+        attended = acc[s] / total[s] + gate_row * (acc[2 + s] / total[2 + s])
         for h in range(4):
             out_ref[s, :, h * D : (h + 1) * D] = attended[:, h * B : (h + 1) * B].T.astype(jnp.bfloat16)
 
-    for cp in img_sends:
+    for cp in img_sends + img_relays:
         cp.wait_send()
     for step in (1, 2, 3):
         x_move(x, x, step).wait_send()
@@ -467,10 +449,9 @@
             pltpu.VMEM((X, 2, 2, D), jnp.bfloat16),
             pltpu.VMEM((8, ZR, X, 2, D), jnp.bfloat16),
             pltpu.VMEM((2, D, ROWS), jnp.bfloat16),
-            pltpu.VMEM((2, D, ROWS), jnp.float32),
-            pltpu.VMEM((2, 1, ROWS), jnp.float32),
-            pltpu.VMEM((2, 1, ROWS), jnp.float32),
-            pltpu.VMEM((2, D, ROWS), jnp.float32),
+            pltpu.VMEM((4, D, ROWS), jnp.float32),
+            pltpu.VMEM((4, 1, ROWS), jnp.float32),
+            pltpu.VMEM((4, 1, ROWS), jnp.float32),
             pltpu.VMEM((2, 1, ROWS), jnp.int32),
             dma((128,)),
             dma((20,)),

time: 76.3 us -> 72.1 us (0.945)
  the two profiles are of different devices: /device:TPU:1017 before, /device:TPU:25 now
where the time goes in v3:
time: 72.1 us; the launch traced here: 70.8 us
  Pallas kernels  67.8 us (94%)
  local copies, waits for them, and re-layouts  1.67 us (2%)
  other arithmetic  1.32 us (2%)
    pallas_call x1, Pallas kernels, per_device(): pl.pallas_call(attention_kernel, out_shape=jax.ShapeDtypeStruct(queries.s...  67.8 us
    unnamed x1, local copies, waits for them, and re-layouts  1.67 us

profile of v3, /device:TPU:25, one launch (start us, length us, event | category | flops | bytes accessed | tf_op | source)
XLA Modules:
  0.0 70.8 jit_solution(9312346513609778398)
XLA Ops:
  0.0 1.3 %reduce = bf16[2048]{0:T(1024)(128)(2,1)} reduce(bf16[1,2048]{1,0:T(2,128)(2,1)} %param.7, bf16[]{:T(256)} %constant.2), dimensions={0}, to_apply=%param.7.reduce_sub_computation | reduce | bytes 8194 | tf_op args[2]
  1.3 67.8 %shard_map.55 = bf16[2,128,512]{2,1,0:T(8,128)(2,1)} custom-call(bf16[2,128,512]{2,1,0:T(8,128)(2,1)} %q_ref.1, bf16[2,128,2048]{2,1,0:T(8,128)(2,1)} %kv_ref.1, bf16[4,2,2,128]{3,2,1,0:T(2,128)(2,1)} %bitcast.2, f32[1,4]{1,0:T(1,128)} %bitcast.3, s32[2]{0:T(128)} %len_ref.1), custom_call_target="tpu_custom_call" | custom-call | tf_op jit(solution)/shard_map/pallas_call | solution.py:436
  69.1 1.7 %copy.7 = bf16[2,128,512]{2,1,0:T(8,128)(2,1)} copy(bf16[2,128,512]{2,1,0:T(8,128)(2,1)} %shard_map.55) | data formatting | bytes 524288

commit v4 on v3

--- a/solution.py
+++ b/solution.py
@@ -108,15 +108,15 @@
         pl.semaphore_signal(token, inc=1, device_id=right, device_id_type=MESH)
 
     def x_move(to, src, step):
-        return remote(img_ref.at[to], xrows.at[src], x_send.at[step], x_recv.at[src], x_peer(step))
+        return remote(img_ref.at[to], xrows.at[:, src], x_send.at[step], x_recv.at[src], x_peer(step))
 
     def row_move(to, src):
         return remote(
-            xrows.at[:, to // 16], img_all.at[ctx, src], row_send.at[to], row_recv.at[src], z_line(to)
+            xrows.at[to // 16], img_all.at[ctx, src], row_send.at[to], row_recv.at[src], z_line(to)
         )
 
-    own_x = pltpu.make_async_copy(img_ref.at[x], xrows.at[x], local.at[2])
-    own_z = pltpu.make_async_copy(xrows.at[:, zp // 16], img_all.at[ctx, zp], local.at[3])
+    own_x = pltpu.make_async_copy(img_ref.at[x], xrows.at[:, x], local.at[2])
+    own_z = pltpu.make_async_copy(xrows.at[zp // 16], img_all.at[ctx, zp], local.at[3])
 
     def rows_down():
         for step in (1, 2, 3):
@@ -285,8 +285,8 @@
         z_step(d, 1)
 
     start_rows()
+    gather_steps(1)
     rows_down()
-    gather_steps(1)
     rows_down_late()
     gather_steps(2)
     y_item(z, 0)
@@ -389,7 +389,7 @@
         fold([(keys, values, None)] * 2, 2)
 
     for s in (0, 1):
-        attended = acc[s] / total[s] + gate_row * (acc[2 + s] / total[2 + s])
+        attended = acc[s] * (1.0 / total[s]) + acc[2 + s] * (gate_row / total[2 + s])
         for h in range(4):
             out_ref[s, :, h * D : (h + 1) * D] = attended[:, h * B : (h + 1) * B].T.astype(jnp.bfloat16)
 
@@ -446,7 +446,7 @@
         out_specs=vmem,
         scratch_shapes=[
             pltpu.VMEM((2, 64 * B, 2 * D), jnp.bfloat16),
-            pltpu.VMEM((X, 2, 2, D), jnp.bfloat16),
+            pltpu.VMEM((2, X, 2, D), jnp.bfloat16),
             pltpu.VMEM((8, ZR, X, 2, D), jnp.bfloat16),
             pltpu.VMEM((2, D, ROWS), jnp.bfloat16),
             pltpu.VMEM((4, D, ROWS), jnp.float32),

time: 72.1 us -> 71.4 us (level)
  no operation moved by 1% of the time
where the time goes in v4:
time: 71.4 us; the launch traced here: 70.1 us
  Pallas kernels  67.1 us (94%)
  local copies, waits for them, and re-layouts  1.67 us (2%)
  other arithmetic  1.32 us (2%)
    pallas_call x1, Pallas kernels, per_device(): pl.pallas_call(attention_kernel, out_shape=jax.ShapeDtypeStruct(queries.s...  67.1 us
    unnamed x1, local copies, waits for them, and re-layouts  1.67 us

profile of v4, /device:TPU:25, one launch (start us, length us, event | category | flops | bytes accessed | tf_op | source)
XLA Modules:
  0.0 70.1 jit_solution(5751802856516623610)
XLA Ops:
  0.0 1.3 %reduce = bf16[2048]{0:T(1024)(128)(2,1)} reduce(bf16[1,2048]{1,0:T(2,128)(2,1)} %param.7, bf16[]{:T(256)} %constant.2), dimensions={0}, to_apply=%param.7.reduce_sub_computation | reduce | bytes 8194 | tf_op args[2]
  1.3 67.1 %shard_map.55 = bf16[2,128,512]{2,1,0:T(8,128)(2,1)} custom-call(bf16[2,128,512]{2,1,0:T(8,128)(2,1)} %q_ref.1, bf16[2,128,2048]{2,1,0:T(8,128)(2,1)} %kv_ref.1, bf16[4,2,2,128]{3,2,1,0:T(2,128)(2,1)} %bitcast.2, f32[1,4]{1,0:T(1,128)} %bitcast.3, s32[2]{0:T(128)} %len_ref.1), custom_call_target="tpu_custom_call" | custom-call | tf_op jit(solution)/shard_map/pallas_call | solution.py:436
  68.4 1.7 %copy.7 = bf16[2,128,512]{2,1,0:T(8,128)(2,1)} copy(bf16[2,128,512]{2,1,0:T(8,128)(2,1)} %shard_map.55) | data formatting | bytes 524288
